TPU v7x, 256 devices: a whole 4x4x8 slice. The times are simulated.
256 devices in a mesh: dp: 64 (over z_hi, x, y, core), fsdp: 4 (over z_lo).
Axes of the slice: x: 4, y: 4, z: 8 (z_hi: 2, z_lo: 4; z = z_hi * 4 + z_lo), core: 2. Of those that a mesh axis runs over, the one named last changes fastest.
Arguments:
- student_tiles: bfloat16 [32768, 16, 256], P(('dp', 'fsdp')), may hold values from -6 to 6
- teacher_tiles: bfloat16 [32768, 16, 512], P(('dp', 'fsdp')), may hold values from -6 to 6
- send_list: int32 [64, 4, 128], P('dp', 'fsdp'), may hold values from -1 to 127, as said below
- clip_weight: float32 [32768], P(('dp', 'fsdp')), may hold values from 0.5 to 64, as said below
- kernel_dilated: bfloat16 [1792, 256], P('fsdp'), may hold values from -0.125 to 0.125
- kernel_mix: bfloat16 [256, 256], P('fsdp'), may hold values from -0.375 to 0.375
- kernel_down: bfloat16 [4096, 512], P('fsdp'), may hold values from -0.09375 to 0.09375
- kernel_proj: bfloat16 [512, 1024], P('fsdp'), may hold values from -0.25 to 0.25
- kernel_teacher: bfloat16 [16, 512, 1024], P(None, 'fsdp'), may hold values from -0.0625 to 0.0625
- alpha_one: float32 [256], replicated, may hold values from 0.5 to 2
- alpha_two: float32 [256], replicated, may hold values from 0.5 to 2
- alpha_three: float32 [256], replicated, may hold values from 0.5 to 2
- alpha_teacher: float32 [512], replicated, may hold values from 0.5 to 2
Outputs:
- student_latent: bfloat16 [32768, 2, 1024], P(('dp', 'fsdp'))
- grad_dilated: float32 [458752], P(('dp', 'fsdp'))
- grad_mix: float32 [65536], P(('dp', 'fsdp'))
- grad_down: float32 [2097152], P(('dp', 'fsdp'))
- grad_proj: float32 [524288], P(('dp', 'fsdp'))
Inputs may be any that keep to these rules, and one draw needn't show every extreme that they name: `send_list`: entries d * 2 .. d * 2 + 1 of a device's list go to dp owner d. Each device's tiles 0 .. L - 1 appear exactly once and no other tile appears, for a count L of 2 to 128 drawn per device; on every device one owner receives 2 tiles, and some device has L = 128. `clip_weight`: positive weights.
All inputs are finite; a program needn't handle non-finite values.
Results may differ from a plain program's by a relative error of at most 0.0067.
Values may be sent and summed in bfloat16 or wider, within the bound.
A program may use at most 128 MiB of HBM per device.

v0:
```python
import jax
import jax.numpy as jnp
from jax import lax
from jax.sharding import PartitionSpec as P

DL = 1024
KS = 16
STRIDE = 8
DILATED_TAPS = 7
UNIT_DILATION = 3
TILE_FRAMES = 16
OUTF = 2


def snake(values, alpha_vec):
    widened = values.astype(jnp.float32)
    return widened + jnp.square(jnp.sin(alpha_vec * widened)) / alpha_vec


def snake_slope(values, alpha_vec):
    return 1.0 + jnp.sin(2.0 * alpha_vec * values)


def unfold_strided(frames):
    tile_count = frames.shape[0]
    margin = (KS - STRIDE) // 2
    padded_frames = jnp.pad(frames, ((0, 0), (margin, margin), (0, 0)))
    windows = [
        padded_frames[:, STRIDE * offset : STRIDE * offset + KS, :].reshape(tile_count, -1)
        for offset in range(OUTF)
    ]
    return jnp.stack(windows, axis=1)


def fold_strided(columns, channels):
    tile_count = columns.shape[0]
    margin = (KS - STRIDE) // 2
    padded_len = TILE_FRAMES + 2 * margin
    pieces = columns.reshape(tile_count, OUTF, KS, channels)
    folded = jnp.zeros((tile_count, padded_len, channels), jnp.float32)
    for offset in range(OUTF):
        folded = folded + jnp.pad(
            pieces[:, offset],
            ((0, 0), (STRIDE * offset, padded_len - KS - STRIDE * offset), (0, 0)),
        )
    return folded[:, margin : margin + TILE_FRAMES, :]


def unfold_dilated(frames):
    tile_count = frames.shape[0]
    receptive_length = UNIT_DILATION * (DILATED_TAPS - 1) // 2
    padded_frames = jnp.pad(frames, ((0, 0), (receptive_length, receptive_length), (0, 0)))
    tap_offsets = [
        padded_frames[
            :, UNIT_DILATION * tap_position : UNIT_DILATION * tap_position + TILE_FRAMES, :
        ]
        for tap_position in range(DILATED_TAPS)
    ]
    return jnp.stack(tap_offsets, axis=2).reshape(tile_count * TILE_FRAMES, -1)


def teacher_forward(tiles, kernel_teacher, alpha_teacher):
    tile_count = tiles.shape[0]
    activated = snake(tiles, alpha_teacher).astype(jnp.bfloat16)
    spread = lax.all_to_all(activated, "fsdp", split_axis=2, concat_axis=0, tiled=True)
    flat_kernel = kernel_teacher.reshape(-1, DL)
    columns = unfold_strided(spread).reshape(tile_count * lax.axis_size("fsdp") * OUTF, -1)
    return lax.psum_scatter(
        jnp.dot(columns, flat_kernel, preferred_element_type=jnp.float32).reshape(
            tile_count * lax.axis_size("fsdp"), OUTF, DL
        ),
        "fsdp",
        scatter_dimension=0,
        tiled=True,
    ).astype(jnp.bfloat16)


def student_step(tiles, target, weights, kernels, alphas):
    kernel_dilated, kernel_mix, kernel_down, kernel_proj = kernels
    alpha_one, alpha_two, alpha_three = alphas
    tile_count = tiles.shape[0]
    channels = tiles.shape[2]
    act_one = snake(tiles, alpha_one).astype(jnp.bfloat16)
    dilated = unfold_dilated(act_one)
    hidden = jnp.dot(dilated, kernel_dilated, preferred_element_type=jnp.float32)
    act_two = snake(hidden, alpha_two).astype(jnp.bfloat16)
    residual = tiles.reshape(tile_count * TILE_FRAMES, channels).astype(jnp.float32) + jnp.dot(
        act_two, kernel_mix, preferred_element_type=jnp.float32
    )
    act_three = (
        snake(residual, alpha_three).astype(jnp.bfloat16).reshape(tile_count, TILE_FRAMES, channels)
    )
    strided = unfold_strided(act_three).reshape(tile_count * OUTF, -1)
    student = jnp.dot(strided, kernel_down, preferred_element_type=jnp.float32).astype(jnp.bfloat16)
    predicted = jnp.dot(student, kernel_proj, preferred_element_type=jnp.float32)
    row_weight = jnp.repeat(weights, OUTF)[:, None]
    error = (
        row_weight
        * (predicted - target.reshape(tile_count * OUTF, DL).astype(jnp.float32))
        / (tile_count * OUTF)
    ).astype(jnp.bfloat16)
    grad_proj = jnp.dot(student.T, error, preferred_element_type=jnp.float32)
    back_student = jnp.dot(error, kernel_proj.T, preferred_element_type=jnp.float32).astype(
        jnp.bfloat16
    )
    grad_down = jnp.dot(strided.T, back_student, preferred_element_type=jnp.float32)
    back_columns = jnp.dot(back_student, kernel_down.T, preferred_element_type=jnp.float32).reshape(
        tile_count, OUTF, -1
    )
    back_three = fold_strided(back_columns, channels).reshape(tile_count * TILE_FRAMES, channels)
    back_residual = (back_three * snake_slope(residual, alpha_three)).astype(jnp.bfloat16)
    grad_mix = jnp.dot(act_two.T, back_residual, preferred_element_type=jnp.float32)
    back_hidden = (
        jnp.dot(back_residual, kernel_mix.T, preferred_element_type=jnp.float32)
        * snake_slope(hidden, alpha_two)
    ).astype(jnp.bfloat16)
    grad_dilated = jnp.dot(dilated.T, back_hidden, preferred_element_type=jnp.float32)
    latent = predicted.astype(jnp.bfloat16).reshape(tile_count, OUTF, DL)
    return (
        latent,
        (
            grad_dilated.reshape(-1),
            grad_mix.reshape(-1),
            grad_down.reshape(-1),
            grad_proj.reshape(-1),
        ),
    )


def on_device(
    student_tiles,
    teacher_tiles,
    send_list,
    clip_weight,
    kernel_dilated,
    kernel_mix,
    kernel_down,
    kernel_proj,
    kernel_teacher,
    alpha_one,
    alpha_two,
    alpha_three,
    alpha_teacher,
):
    routes = send_list.reshape(-1)
    live_rows = (routes >= 0)[:, None, None]
    picked = jnp.maximum(routes, 0)

    def packed(values):
        return jnp.where(live_rows, jnp.take(values, picked, axis=0), jnp.zeros((), values.dtype))

    student_part, teacher_part = (
        lax.all_to_all(packed(student_tiles), "dp", split_axis=0, concat_axis=0, tiled=True),
        lax.all_to_all(packed(teacher_tiles), "dp", split_axis=0, concat_axis=0, tiled=True),
    )
    target = teacher_forward(teacher_part, kernel_teacher, alpha_teacher)
    kernels = (
        lax.all_gather(kernel_dilated, "fsdp", axis=0, tiled=True),
        lax.all_gather(kernel_mix, "fsdp", axis=0, tiled=True),
        lax.all_gather(kernel_down, "fsdp", axis=0, tiled=True),
        lax.all_gather(kernel_proj, "fsdp", axis=0, tiled=True),
    )
    latent, gradients = student_step(
        student_part, target, clip_weight, kernels, (alpha_one, alpha_two, alpha_three)
    )
    gradients = (
        lax.psum_scatter(gradients[0], ("dp", "fsdp"), scatter_dimension=0, tiled=True),
        lax.psum_scatter(gradients[1], ("dp", "fsdp"), scatter_dimension=0, tiled=True),
        lax.psum_scatter(gradients[2], ("dp", "fsdp"), scatter_dimension=0, tiled=True),
        lax.psum_scatter(gradients[3], ("dp", "fsdp"), scatter_dimension=0, tiled=True),
    )
    return (latent, gradients[0], gradients[1], gradients[2], gradients[3])


def solution(mesh):
    placed = (
        P(("dp", "fsdp"), None, None),
        P(("dp", "fsdp"), None, None),
        P("dp", "fsdp", None),
        P(("dp", "fsdp")),
        P("fsdp", None),
        P("fsdp", None),
        P("fsdp", None),
        P("fsdp", None),
        P(None, "fsdp", None),
        P(),
        P(),
        P(),
        P(),
    )
    return jax.shard_map(
        on_device,
        mesh=mesh,
        in_specs=placed,
        out_specs=(
            P(("dp", "fsdp"), None, None),
            P(("dp", "fsdp")),
            P(("dp", "fsdp")),
            P(("dp", "fsdp")),
            P(("dp", "fsdp")),
        ),
        check_vma=False,
    )
```

profile of v0, /device:TPU:8, one launch (start us, length us, event | category | flops | bytes accessed | tf_op | source)
XLA Modules:
  0.0 759.4 jit_solution(11630443974876374161)
XLA Ops:
  13.8 14.7 %all-to-all-start.1 = ((bf16[128,16,512]{2,1,0:T(8,128)(2,1)}), bf16[128,16,512]{2,1,0:T(8,128)(2,1)S(1)}, u32[]{:S(2)}, u32[]{:S(2)}) async-start(bf16[128,16,512]{2,1,0:T(8,128)(2,1)} %select_select_fusion), calls=%async_computation.1 | async-start | bytes 4194304 | tf_op jit(solution)/shard_map/all_to_all | solution.py:154
  29.3 46.7 %all-to-all-done.1 = bf16[128,16,512]{2,1,0:T(8,128)(2,1)S(1)} async-done(((bf16[128,16,512]{2,1,0:T(8,128)(2,1)}), bf16[128,16,512]{2,1,0:T(8,128)(2,1)S(1)}, u32[]{:S(2)}, u32[]{:S(2)}) %all-to-all-start.1) | async-done | bytes 2097184 | tf_op jit(solution)/shard_map/all_to_all | solution.py:154
  75.9 15.0 %fusion.3 = bf16[128,16,512]{2,1,0:T(8,128)(2,1)} fusion(bf16[128,16,512]{2,1,0:T(8,128)(2,1)S(1)} %all-to-all-done.1, f32[512]{0:T(512)S(1)} %copy-done.13), kind=kLoop, calls=%fused_computation.13 | loop fusion | flops 6291456 | bytes 4196352 | tf_op jit(solution)/shard_map/convert_element_type | solution.py:64
  91.0 4.2 copy.52
  95.2 93.7 %all_to_all.28 = bf16[128,16,512]{0,1,2:T(8,128)(2,1)} all-to-all(bf16[128,16,512]{0,1,2:T(8,128)(2,1)S(1)} %copy.52), channel_id=1, replica_groups=mesh['dp'=64,'fsdp'=4] {'fsdp'}, dimensions={2} | all-to-all | bytes 4194304 | tf_op jit(solution)/shard_map/all_to_all | solution.py:65
  189.0 5.1 copy.53
  194.0 5.3 pad_slice_fusion.7
  199.4 4.1 stack_reshape.15
  205.8 10.0 %fusion.4 = f32[512,2,1024]{2,0,1:T(8,128)} fusion(bf16[2048,1024,1]{1,0,2:T(8,128)(2,1)} %bitcast.109, bf16[512,1,2048]{2,0,1:T(8,128)(2,1)} %stack_reshape.15, bf16[512,1,2048]{2,0,1:T(8,128)(2,1)} %stack_reshape.14), kind=kOutput, calls=%fused_computation.14 | convolution fusion | flops 4297064448 | bytes 12582912 | tf_op jit(solution)/shard_map/dot_general | solution.py:69
  219.2 11.7 %all-to-all-start = ((bf16[128,16,256]{2,1,0:T(8,128)(2,1)}), bf16[128,16,256]{2,1,0:T(8,128)(2,1)S(1)}, u32[]{:S(2)}, u32[]{:S(2)}) async-start(bf16[128,16,256]{2,1,0:T(8,128)(2,1)} %select_select_fusion.1), calls=%async_computation | async-start | bytes 2097152 | tf_op jit(solution)/shard_map/all_to_all | solution.py:153
  232.0 56.0 %all_gather.13 = bf16[256,256]{1,0:T(8,128)(2,1)S(1)} all-gather(bf16[64,256]{1,0:T(8,128)(2,1)S(1)} %copy-done.11), channel_id=1, replica_groups=mesh['dp'=64,'fsdp'=4] {'fsdp'}, dimensions={0}, use_global_device_ids=true | all-gather | bytes 163840 | tf_op jit(solution)/shard_map/all_gather | solution.py:159
  288.0 34.1 %all_gather.12 = bf16[1792,256]{1,0:T(8,128)(2,1)} all-gather(bf16[448,256]{1,0:T(8,128)(2,1)S(1)} %copy-done.10), channel_id=1, replica_groups=mesh['dp'=64,'fsdp'=4] {'fsdp'}, dimensions={0}, use_global_device_ids=true | all-gather | bytes 1146880 | tf_op jit(solution)/shard_map/all_gather | solution.py:158
  322.1 7.3 add_convert_fusion.2
  333.4 7.9 %bitcast_dynamic-update-slice_fusion = bf16[128,16,7,256]{3,1,0,2:T(8,128)(2,1)} fusion(bf16[128,16,7,256]{3,1,0,2:T(8,128)(2,1)} %fusion.15, f32[256]{0:T(256)S(1)} %copy-done.12, bf16[128,16,256]{2,1,0:T(8,128)(2,1)S(1)} %all-to-all-done), kind=kLoop, calls=%fused_computation.53 | loop fusion | flops 3145728 | bytes 2098176
  345.3 14.4 %copy.49 = bf16[128,16,7,256]{3,2,1,0:T(8,128)(2,1)} copy(bf16[128,16,7,256]{3,1,0,2:T(8,128)(2,1)} %fusion.21) | data formatting | bytes 14680064 | tf_op jit(solution)/shard_map/stack | solution.py:59
  359.8 7.2 copy.59
  369.9 15.2 %add_convert_fusion = (bf16[2048,256]{1,0:T(8,128)(2,1)S(1)}, f32[2048,256]{1,0:T(8,128)}) fusion(f32[256]{0:T(256)S(1)} %copy-done.14, bf16[256,256]{1,0:T(8,128)(2,1)S(1)} %all_gather.13, f32[2048,256]{1,0:T(8,128)S(1)} %fusion.26, f32[256]{0:T(256)S(1)} %copy-done.15, bf16[2048,256]{1,0:T(8,128)(2,1)S(1)} %bitcast.98), kind=kOutput, calls=%fused_computation.31 | convolution fusion | flops 274726912 | bytes 6424576 | tf_op jit(solution)/shard_map/dot_general | solution.py:87
  386.6 4.0 copy.51
  406.9 4.5 convolution_bitcast_fusion
  416.6 7.2 fusion.9
  423.8 7.6 %convolution_bitcast_fusion.3 = f32[32,2,8,128]{3,2,1,0:T(8,128)S(1)} fusion(bf16[2048,256]{1,0:T(8,128)(2,1)S(1)} %fusion.9, f32[2048,256]{1,0:T(8,128)S(1)} %copy-done.18, f32[256]{0:T(256)S(1)} %copy-done.15), kind=kOutput, calls=%fused_computation.40 | convolution fusion | flops 271056896 | bytes 3408896 | tf_op jit(solution)/shard_map/dot_general | solution.py:112
  431.5 12.2 %convolution_bitcast_fusion.2 = f32[224,2,8,128]{3,2,1,0:T(8,128)S(1)} fusion(bf16[2048,1792]{1,0:T(8,128)(2,1)} %bitcast.104, bf16[2048,256]{1,0:T(8,128)(2,1)S(1)} %fusion.9, bf16[256,256]{1,0:T(8,128)(2,1)S(1)} %all_gather.13, f32[2048,256]{1,0:T(8,128)} %copy-done.17, f32[256]{0:T(256)S(1)} %broadcast_multiply_fusion), kind=kOutput, calls=%fused_computation.37 | convolution fusion | flops 2149580800 | bytes 12452864 | tf_op jit(solution)/shard_map/dot_general | solution.py:117
  446.7 9.0 %copy.63 = f32[512,4,8,128]{3,1,2,0:T(4,128)} copy(f32[512,4,8,128]{3,2,1,0:T(8,128)} %convolution_bitcast_fusion) | data formatting | bytes 16777216
  459.5 287.5 %all-reduce.12.cloned.1.call-done = (f32[458752]{0:T(1024)}, f32[65536]{0:T(1024)}, f32[2097152]{0:T(1024)}, f32[524288]{0:T(1024)}) async-done(((f32[458752]{0:T(1024)}, f32[65536]{0:T(1024)}, f32[2097152]{0:T(1024)}, f32[524288]{0:T(1024)}), (f32[458752]{0:T(1024)}, f32[65536]{0:T(1024)}, f32[2097152]{0:T(1024)}, f32[524288]{0:T(1024)})) %all-reduce.12.cloned.1.call-update) | async-done | bytes 12582928
  (92 shorter events, 60.2 us)
Async XLA Ops:
  7.2 1.6 copy-start
  13.8 62.2 %copy-start.13 = (f32[512]{0:T(512)S(1)}, f32[512]{0:T(512)}, u32[]{:S(2)}) copy-start(f32[512]{0:T(512)} %param.25) | copy-start | bytes 6148
  13.8 62.2 %all-to-all-start.1 = ((bf16[128,16,512]{2,1,0:T(8,128)(2,1)}), bf16[128,16,512]{2,1,0:T(8,128)(2,1)S(1)}, u32[]{:S(2)}, u32[]{:S(2)}) async-start(bf16[128,16,512]{2,1,0:T(8,128)(2,1)} %select_select_fusion), calls=%async_computation.1 | async-start | bytes 4194304 | tf_op jit(solution)/shard_map/all_to_all | solution.py:154
  28.5 365.0 %all-gather.3.cloned.1.call-start = ((), (), s32[]{:S(2)}) async-start(), calls=%async_computation.4 | async-start | bytes 5242880 | tf_op jit(solution)/shard_map/all_gather | solution.py:160
  29.2 367.8 %reduce-scatter.2.cloned.1.call-start = ((), (), s32[]{:S(2)}) async-start(), calls=%async_computation.6 | async-start | bytes 5242880 | tf_op jit(solution)/shard_map/reduce_scatter | solution.py:68
  215.8 1.2 copy-start.8
  217.7 14.1 %copy-start.16 = (f32[128]{0:T(128)S(1)}, f32[128]{0:T(128)}, u32[]{:S(2)}) copy-start(f32[128]{0:T(128)} %param.16) | copy-start | bytes 1540
  217.7 14.3 %copy-start.11 = (bf16[64,256]{1,0:T(8,128)(2,1)S(1)}, bf16[64,256]{1,0:T(8,128)(2,1)}, u32[]{:S(2)}) copy-start(bf16[64,256]{1,0:T(8,128)(2,1)} %param.18) | copy-start | bytes 98308
  217.7 70.3 %copy-start.14 = (f32[256]{0:T(256)S(1)}, f32[256]{0:T(256)}, u32[]{:S(2)}) copy-start(f32[256]{0:T(256)} %param.24) | copy-start | bytes 3076
  217.7 70.3 %copy-start.15 = (f32[256]{0:T(256)S(1)}, f32[256]{0:T(256)}, u32[]{:S(2)}) copy-start(f32[256]{0:T(256)} %param.23) | copy-start | bytes 3076
  217.7 70.3 %copy-start.10 = (bf16[448,256]{1,0:T(8,128)(2,1)S(1)}, bf16[448,256]{1,0:T(8,128)(2,1)}, u32[]{:S(2)}) copy-start(bf16[448,256]{1,0:T(8,128)(2,1)} %param.17) | copy-start | bytes 688132
  219.2 102.9 %copy-start.12 = (f32[256]{0:T(256)S(1)}, f32[256]{0:T(256)}, u32[]{:S(2)}) copy-start(f32[256]{0:T(256)} %param.22) | copy-start | bytes 3076
  219.2 102.8 %all-to-all-start = ((bf16[128,16,256]{2,1,0:T(8,128)(2,1)}), bf16[128,16,256]{2,1,0:T(8,128)(2,1)S(1)}, u32[]{:S(2)}, u32[]{:S(2)}) async-start(bf16[128,16,256]{2,1,0:T(8,128)(2,1)} %select_select_fusion.1), calls=%async_computation | async-start | bytes 2097152 | tf_op jit(solution)/shard_map/all_to_all | solution.py:153
  230.9 171.1 %all-gather.5.cloned.1.call-start = ((), (), s32[]{:S(2)}) async-start(), calls=%async_computation.5 | async-start | bytes 1310720 | tf_op jit(solution)/shard_map/all_gather | solution.py:161
  231.7 515.4 %all-reduce.12.cloned.1.call-start = ((), (), s32[]{:S(2)}) async-start(), calls=%async_computation.7 | async-start | bytes 25165824
  359.8 7.2 copy-start.9
  366.9 2.9 copy-start.3
  369.9 15.2 %copy-start.17 = (f32[2048,256]{1,0:T(8,128)}, f32[2048,256]{1,0:T(8,128)S(1)}, u32[]{:S(2)}) copy-start(f32[2048,256]{1,0:T(8,128)S(1)} %fusion.26) | copy-start | bytes 6291460
  404.6 1.8 copy-start.4
  406.9 4.6 copy-start.5
  415.0 1.6 copy-start.7
  416.6 7.2 copy-start.18
  446.7 9.0 %copy-start.2 = (f32[64,8,8,128]{3,2,1,0:T(8,128)S(1)}, f32[64,8,8,128]{3,2,1,0:T(8,128)}, u32[]{:S(2)}) copy-start(f32[64,8,8,128]{3,2,1,0:T(8,128)} %convolution_bitcast_fusion.1) | copy-start | bytes 6291460
  457.5 294.9 %copy-start.1 = (bf16[128,16,512]{2,1,0:T(8,128)(2,1)S(1)}, bf16[128,16,512]{2,1,0:T(8,128)(2,1)}, u32[]{:S(2)}) copy-start(bf16[128,16,512]{2,1,0:T(8,128)(2,1)} %param.14) | copy-start | bytes 6291460
  (1 other events, 1.0 us)
Sparse Core Ops, SparseCore 0:
  31.1 111.8 all-gather.2
  215.9 121.1 reduce-scatter.1
  339.0 33.9 all-gather.4
  457.7 289.3 all-reduce.11
where the time goes:
time: 769 us; the launch traced here: 759 us
  waiting for transfers between devices  336 us (44%)
  blocking collectives  184 us (24%)
  local copies, waits for them, and re-layouts  92.4 us (12%)
  matrix products  61.1 us (8%)
  other arithmetic  45.3 us (6%)
  starting transfers between devices  26.6 us (3%)
  between operations  14.5 us (2%)
    unnamed x5, waiting for transfers between devices  289 us
    all_to_all x1, blocking collectives, teacher_forward(): lax.all_to_all(activated, 'fsdp', split_axis=2, concat_axis=0, tiled=True)  93.7 us
    all_gather x1, blocking collectives, on_device(): lax.all_gather(kernel_mix, 'fsdp', axis=0, tiled=True)  56 us
    all_to_all x1, waiting for transfers between devices, on_device(): lax.all_to_all(packed(teacher_tiles), 'dp', split_axis=0, concat_axis=0,...  46.7 us
    unnamed x53, local copies, waits for them, and re-layouts  39.3 us
    all_gather x1, blocking collectives, on_device(): lax.all_gather(kernel_dilated, 'fsdp', axis=0, tiled=True)  34.1 us
    another operation x2, local copies, waits for them, and re-layouts, unfold_dilated(): return jnp.stack(tap_offsets, axis=2).reshape(tile_count * TILE_FRAMES, -1)  15.6 us
  transfers between devices with their start and end apart: 6, of which 2 were waited for; matrix products, arithmetic and copies ran while one was open for 17% of the time, Pallas kernels for 0%

commit v1 on v0

--- a/solution.py
+++ b/solution.py
@@ -10,6 +10,11 @@
 UNIT_DILATION = 3
 TILE_FRAMES = 16
 OUTF = 2
+
+
+def swapped_in(x, name, dim):
+    sent = jnp.stack([x] * lax.axis_size(name))
+    return jnp.concatenate(lax.all_to_all(sent, name, 0, 0), axis=dim)
 
 
 def snake(values, alpha_vec):
@@ -156,7 +161,7 @@
     target = teacher_forward(teacher_part, kernel_teacher, alpha_teacher)
     kernels = (
         lax.all_gather(kernel_dilated, "fsdp", axis=0, tiled=True),
-        lax.all_gather(kernel_mix, "fsdp", axis=0, tiled=True),
+        swapped_in(kernel_mix, "fsdp", 0),
         lax.all_gather(kernel_down, "fsdp", axis=0, tiled=True),
         lax.all_gather(kernel_proj, "fsdp", axis=0, tiled=True),
     )

time: 769 us -> 765 us (level)
  blocking collectives: 184 us -> 169 us
    all_gather x1 -> x0, blocking collectives: 56 us -> none  [on_device(): lax.all_gather(kernel_mix, 'fsdp', axis=0, tiled=True)]
    all_gather x1, blocking collectives: 34.1 us -> 74.8 us  [on_device(): lax.all_gather(kernel_dilated, 'fsdp', axis=0, tiled=True)]
    unnamed x53 -> x51, local copies, waits for them, and re-layouts: 39.3 us -> 41.6 us
  transfers between devices with their start and end apart: 6 -> 7, of which waited for: 2 -> 2; matrix products, arithmetic and copies ran while one was open for 17% -> 18% of each run, Pallas kernels for 0% -> 0%
where the time goes in v1:
time: 765 us; the launch traced here: 755 us
  waiting for transfers between devices  337 us (44%)
  blocking collectives  169 us (22%)
  local copies, waits for them, and re-layouts  95.5 us (12%)
  matrix products  63.8 us (8%)
  other arithmetic  45.3 us (6%)
  starting transfers between devices  30.5 us (4%)
  between operations  14.5 us (2%)
    unnamed x5, waiting for transfers between devices  290 us
    all_to_all x1, blocking collectives, teacher_forward(): lax.all_to_all(activated, 'fsdp', split_axis=2, concat_axis=0, tiled=True)  93.7 us
    all_gather x1, blocking collectives, on_device(): lax.all_gather(kernel_dilated, 'fsdp', axis=0, tiled=True)  74.8 us
    all_to_all x1, waiting for transfers between devices, on_device(): lax.all_to_all(packed(teacher_tiles), 'dp', split_axis=0, concat_axis=0,...  46.7 us
    unnamed x51, local copies, waits for them, and re-layouts  41.6 us
    dot_general x1, matrix products, student_step(): jnp.dot(act_two, kernel_mix, preferred_element_type=jnp.float32)  16.5 us
    another operation x2, local copies, waits for them, and re-layouts, unfold_dilated(): return jnp.stack(tap_offsets, axis=2).reshape(tile_count * TILE_FRAMES, -1)  15.6 us
  transfers between devices with their start and end apart: 7, of which 2 were waited for; matrix products, arithmetic and copies ran while one was open for 18% of the time, Pallas kernels for 0%

profile of v1, /device:TPU:8, one launch (start us, length us, event | category | flops | bytes accessed | tf_op | source)
XLA Modules:
  0.0 754.9 jit_solution(17764694372731030763)
XLA Ops:
  13.8 14.7 %all-to-all-start.2 = ((bf16[128,16,512]{2,1,0:T(8,128)(2,1)}), bf16[128,16,512]{2,1,0:T(8,128)(2,1)S(1)}, u32[]{:S(2)}, u32[]{:S(2)}) async-start(bf16[128,16,512]{2,1,0:T(8,128)(2,1)} %select_select_fusion), calls=%async_computation.2 | async-start | bytes 4194304 | tf_op jit(solution)/shard_map/all_to_all | solution.py:159
  29.3 46.7 %all-to-all-done.2 = bf16[128,16,512]{2,1,0:T(8,128)(2,1)S(1)} async-done(((bf16[128,16,512]{2,1,0:T(8,128)(2,1)}), bf16[128,16,512]{2,1,0:T(8,128)(2,1)S(1)}, u32[]{:S(2)}, u32[]{:S(2)}) %all-to-all-start.2) | async-done | bytes 2097184 | tf_op jit(solution)/shard_map/all_to_all | solution.py:159
  76.0 15.0 %fusion.3 = bf16[128,16,512]{2,1,0:T(8,128)(2,1)} fusion(bf16[128,16,512]{2,1,0:T(8,128)(2,1)S(1)} %all-to-all-done.2, f32[512]{0:T(512)S(1)} %copy-done.13), kind=kLoop, calls=%fused_computation.13 | loop fusion | flops 6291456 | bytes 4196352 | tf_op jit(solution)/shard_map/convert_element_type | solution.py:69
  91.0 4.2 copy.52
  95.2 93.7 %all_to_all.33 = bf16[128,16,512]{0,1,2:T(8,128)(2,1)} all-to-all(bf16[128,16,512]{0,1,2:T(8,128)(2,1)S(1)} %copy.52), channel_id=1, replica_groups=mesh['dp'=64,'fsdp'=4] {'fsdp'}, dimensions={2} | all-to-all | bytes 4194304 | tf_op jit(solution)/shard_map/all_to_all | solution.py:70
  189.0 5.1 copy.53
  194.1 5.3 pad_slice_fusion.7
  199.4 4.2 stack_reshape.15
  205.9 10.0 %fusion.4 = f32[512,2,1024]{2,0,1:T(8,128)} fusion(bf16[2048,1024,1]{1,0,2:T(8,128)(2,1)} %bitcast.112, bf16[512,1,2048]{2,0,1:T(8,128)(2,1)} %stack_reshape.15, bf16[512,1,2048]{2,0,1:T(8,128)(2,1)} %stack_reshape.14), kind=kOutput, calls=%fused_computation.14 | convolution fusion | flops 4297064448 | bytes 12582912 | tf_op jit(solution)/shard_map/dot_general | solution.py:74
  219.3 11.7 %all-to-all-start = ((bf16[128,16,256]{2,1,0:T(8,128)(2,1)}), bf16[128,16,256]{2,1,0:T(8,128)(2,1)S(1)}, u32[]{:S(2)}, u32[]{:S(2)}) async-start(bf16[128,16,256]{2,1,0:T(8,128)(2,1)} %select_select_fusion.1), calls=%async_computation | async-start | bytes 2097152 | tf_op jit(solution)/shard_map/all_to_all | solution.py:158
  232.0 74.8 %all_gather.9 = bf16[1792,256]{1,0:T(8,128)(2,1)} all-gather(bf16[448,256]{1,0:T(8,128)(2,1)S(1)} %copy-done.10), channel_id=1, replica_groups=mesh['dp'=64,'fsdp'=4] {'fsdp'}, dimensions={0}, use_global_device_ids=true | all-gather | bytes 1146880 | tf_op jit(solution)/shard_map/all_gather | solution.py:163
  307.5 4.0 all-to-all-start.1
  311.5 7.3 add_convert_fusion.2
  322.8 7.8 %bitcast_dynamic-update-slice_fusion = bf16[128,16,7,256]{3,1,0,2:T(8,128)(2,1)} fusion(bf16[128,16,7,256]{3,1,0,2:T(8,128)(2,1)} %fusion.15, f32[256]{0:T(256)S(1)} %copy-done.12, bf16[128,16,256]{2,1,0:T(8,128)(2,1)S(1)} %all-to-all-done), kind=kLoop, calls=%fused_computation.53 | loop fusion | flops 3145728 | bytes 2098176
  334.7 14.5 %copy.49 = bf16[128,16,7,256]{3,2,1,0:T(8,128)(2,1)} copy(bf16[128,16,7,256]{3,1,0,2:T(8,128)(2,1)} %fusion.21) | data formatting | bytes 14680064 | tf_op jit(solution)/shard_map/stack | solution.py:64
  349.2 7.3 copy.59
  363.0 16.5 %add_convert_fusion = (bf16[2048,256]{1,0:T(8,128)(2,1)S(1)}, f32[2048,256]{1,0:T(8,128)}) fusion(f32[256]{0:T(256)S(1)} %copy-done.14, bf16[256,256]{1,0:T(8,128)(2,1)S(1)} %bitcast.110, f32[2048,256]{1,0:T(8,128)} %fusion.26, f32[256]{0:T(256)S(1)} %copy-done.15, bf16[2048,256]{1,0:T(8,128)(2,1)S(1)} %bitcast.99), kind=kOutput, calls=%fused_computation.31 | convolution fusion | flops 274726912 | bytes 6424576 | tf_op jit(solution)/shard_map/dot_general | solution.py:92
  381.1 4.0 copy.51
  401.4 4.5 convolution_bitcast_fusion
  411.1 7.2 fusion.9
  418.3 7.6 %convolution_bitcast_fusion.3 = f32[32,2,8,128]{3,2,1,0:T(8,128)S(1)} fusion(bf16[2048,256]{1,0:T(8,128)(2,1)S(1)} %fusion.9, f32[2048,256]{1,0:T(8,128)S(1)} %copy-done.17, f32[256]{0:T(256)S(1)} %copy-done.15), kind=kOutput, calls=%fused_computation.40 | convolution fusion | flops 271056896 | bytes 3408896 | tf_op jit(solution)/shard_map/dot_general | solution.py:117
  425.9 12.2 %convolution_bitcast_fusion.2 = f32[224,2,8,128]{3,2,1,0:T(8,128)S(1)} fusion(bf16[2048,1792]{1,0:T(8,128)(2,1)} %bitcast.105, bf16[2048,256]{1,0:T(8,128)(2,1)S(1)} %fusion.9, bf16[256,256]{1,0:T(8,128)(2,1)S(1)} %bitcast.111, f32[2048,256]{1,0:T(8,128)} %fusion.26, f32[256]{0:T(256)S(1)} %broadcast_multiply_fusion), kind=kOutput, calls=%fused_computation.37 | convolution fusion | flops 2149580800 | bytes 12452864 | tf_op jit(solution)/shard_map/dot_general | solution.py:122
  441.2 9.0 %copy.63 = f32[512,4,8,128]{3,1,2,0:T(4,128)} copy(f32[512,4,8,128]{3,2,1,0:T(8,128)} %convolution_bitcast_fusion) | data formatting | bytes 16777216
  454.0 288.7 %all-reduce.12.cloned.1.call-done = (f32[458752]{0:T(1024)}, f32[65536]{0:T(1024)}, f32[2097152]{0:T(1024)}, f32[524288]{0:T(1024)}) async-done(((f32[458752]{0:T(1024)}, f32[65536]{0:T(1024)}, f32[2097152]{0:T(1024)}, f32[524288]{0:T(1024)}), (f32[458752]{0:T(1024)}, f32[65536]{0:T(1024)}, f32[2097152]{0:T(1024)}, f32[524288]{0:T(1024)})) %all-reduce.12.cloned.1.call-update) | async-done | bytes 12582928
  (92 shorter events, 64.4 us)
Async XLA Ops:
  7.2 1.6 copy-start
  13.8 62.2 %copy-start.13 = (f32[512]{0:T(512)S(1)}, f32[512]{0:T(512)}, u32[]{:S(2)}) copy-start(f32[512]{0:T(512)} %param.25) | copy-start | bytes 6148
  13.8 62.2 %all-to-all-start.2 = ((bf16[128,16,512]{2,1,0:T(8,128)(2,1)}), bf16[128,16,512]{2,1,0:T(8,128)(2,1)S(1)}, u32[]{:S(2)}, u32[]{:S(2)}) async-start(bf16[128,16,512]{2,1,0:T(8,128)(2,1)} %select_select_fusion), calls=%async_computation.2 | async-start | bytes 4194304 | tf_op jit(solution)/shard_map/all_to_all | solution.py:159
  28.5 359.5 %all-gather.3.cloned.1.call-start = ((), (), s32[]{:S(2)}) async-start(), calls=%async_computation.5 | async-start | bytes 5242880 | tf_op jit(solution)/shard_map/all_gather | solution.py:165
  29.2 362.2 %reduce-scatter.2.cloned.1.call-start = ((), (), s32[]{:S(2)}) async-start(), calls=%async_computation.7 | async-start | bytes 5242880 | tf_op jit(solution)/shard_map/reduce_scatter | solution.py:73
  215.8 1.2 copy-start.8
  217.7 14.0 %copy-start.16 = (f32[128]{0:T(128)S(1)}, f32[128]{0:T(128)}, u32[]{:S(2)}) copy-start(f32[128]{0:T(128)} %param.16) | copy-start | bytes 1540
  217.7 14.3 %copy-start.14 = (f32[256]{0:T(256)S(1)}, f32[256]{0:T(256)}, u32[]{:S(2)}) copy-start(f32[256]{0:T(256)} %param.24) | copy-start | bytes 3076
  217.7 14.3 %copy-start.15 = (f32[256]{0:T(256)S(1)}, f32[256]{0:T(256)}, u32[]{:S(2)}) copy-start(f32[256]{0:T(256)} %param.23) | copy-start | bytes 3076
  217.7 14.3 %copy-start.10 = (bf16[448,256]{1,0:T(8,128)(2,1)S(1)}, bf16[448,256]{1,0:T(8,128)(2,1)}, u32[]{:S(2)}) copy-start(bf16[448,256]{1,0:T(8,128)(2,1)} %param.17) | copy-start | bytes 688132
  219.3 87.5 %copy-start.11 = (bf16[64,256]{1,0:T(8,128)(2,1)S(1)}, bf16[64,256]{1,0:T(8,128)(2,1)}, u32[]{:S(2)}) copy-start(bf16[64,256]{1,0:T(8,128)(2,1)} %param.18) | copy-start | bytes 98308
  219.3 92.2 %copy-start.12 = (f32[256]{0:T(256)S(1)}, f32[256]{0:T(256)}, u32[]{:S(2)}) copy-start(f32[256]{0:T(256)} %param.22) | copy-start | bytes 3076
  219.3 87.5 %all-to-all-start = ((bf16[128,16,256]{2,1,0:T(8,128)(2,1)}), bf16[128,16,256]{2,1,0:T(8,128)(2,1)S(1)}, u32[]{:S(2)}, u32[]{:S(2)}) async-start(bf16[128,16,256]{2,1,0:T(8,128)(2,1)} %select_select_fusion.1), calls=%async_computation | async-start | bytes 2097152 | tf_op jit(solution)/shard_map/all_to_all | solution.py:158
  231.0 165.6 %all-gather.5.cloned.1.call-start = ((), (), s32[]{:S(2)}) async-start(), calls=%async_computation.6 | async-start | bytes 1310720 | tf_op jit(solution)/shard_map/all_gather | solution.py:166
  307.5 55.5 %all-to-all-start.1 = ((bf16[4,64,256]{2,1,0:T(8,128)(2,1)}), bf16[4,64,256]{2,1,0:T(8,128)(2,1)S(1)}, u32[]{:S(2)}, u32[]{:S(2)}) async-start(bf16[4,64,256]{2,1,0:T(8,128)(2,1)} %stack.45), calls=%async_computation.1 | async-start | bytes 262144 | tf_op jit(solution)/shard_map/all_to_all | solution.py:17
  311.5 431.2 %all-reduce.12.cloned.1.call-start = ((), (), s32[]{:S(2)}) async-start(), calls=%async_computation.8 | async-start | bytes 25165824
  349.2 10.3 %copy-start.9 = (bf16[1792,256]{1,0:T(8,128)(2,1)S(1)}, bf16[1792,256]{1,0:T(8,128)(2,1)}, u32[]{:S(2)}) copy-start(bf16[1792,256]{1,0:T(8,128)(2,1)} %all_gather.9) | copy-start | bytes 2752516
  356.6 2.9 copy-start.3
  399.0 1.8 copy-start.4
  401.4 4.6 copy-start.5
  409.5 1.6 copy-start.7
  411.1 7.2 copy-start.17
  441.2 9.0 %copy-start.2 = (f32[64,8,8,128]{3,2,1,0:T(8,128)S(1)}, f32[64,8,8,128]{3,2,1,0:T(8,128)}, u32[]{:S(2)}) copy-start(f32[64,8,8,128]{3,2,1,0:T(8,128)} %convolution_bitcast_fusion.1) | copy-start | bytes 6291460
  452.0 296.1 %copy-start.1 = (bf16[128,16,512]{2,1,0:T(8,128)(2,1)S(1)}, bf16[128,16,512]{2,1,0:T(8,128)(2,1)}, u32[]{:S(2)}) copy-start(bf16[128,16,512]{2,1,0:T(8,128)(2,1)} %param.14) | copy-start | bytes 6291460
  (1 other events, 1.0 us)
Sparse Core Ops, SparseCore 0:
  31.1 111.8 all-gather.2
  216.0 121.1 reduce-scatter.1
  339.0 33.9 all-gather.4
  452.1 290.5 all-reduce.11
